TPU v7x, 32 devices: a whole 2x2x4 slice. The times are simulated.
32 devices in a mesh: dom: 16 (over z, y, x), orb: 2 (over core).
Axes of the slice: x: 2, y: 2, z: 4, core: 2. Of those that a mesh axis runs over, the one named last changes fastest.
Arguments:
- orbitals: bfloat16 [768, 64, 512], P('dom', 'orb'), may hold values from -6 to 6
- adjoint_source: bfloat16 [768, 64, 512], P('dom', 'orb'), may hold values from -6 to 6
- eigenvalues: float32 [64], P('orb'), may hold values from -1 to -0.25
- cell_scale: float32 [768], P('dom'), may hold values from 0.4 to 1.6
- base_potential: float32 [768, 512], P('dom'), may hold values from 0.5 to 1.5
- stiffness: bfloat16 [512, 512], replicated, may hold values from -1.5 to 1.5, as said below
- face_perm: int32 [768, 64], P('dom'), may hold values from 0 to 63, each once within a row
- restrict: bfloat16 [512, 64], replicated, may hold values from -0.25 to 0.25
- prolong: bfloat16 [64, 512], replicated, may hold values from -0.75 to 0.75
- owner: int32 [768, 1], P('dom'), may hold values from 0 to 15; in each aligned block of 48 rows (0 to 47, 48 to 95, ...) at most 6 rows name the same one
- pot_slot: int32 [768], P('dom'), may hold values from 0 to 63
- potential: float32 [1024, 64], P('dom'), may hold values from -6 to 6
Outputs:
- adjoint: bfloat16 [768, 64, 512], P('dom', 'orb')
- updated: float32 [1024, 64], P('dom')
- applied: bfloat16 [768, 64, 512], P('dom', 'orb')
Inputs may be any that keep to these rules, and one draw needn't show every extreme that they name: In the rows of one device no owner is named by more than 6 cells. `face_perm`: each row is a permutation. `stiffness`: symmetric.
All inputs are finite; a program needn't handle non-finite values.
Results may differ from a plain program's by a relative error of at most 0.0027.
Values sent between devices are 32-bit elements; how exact they have to be, the bound alone decides.
A program may use at most 64 MiB of HBM per device.

v0:
```python
import jax
import jax.numpy as jnp
from jax import lax
from jax.sharding import PartitionSpec as P

ITERS = 4
relax = 0.25
step_rate = 0.1


def padded_2(block, sides, width):
    for axis, dim in sides:
        count = lax.axis_size(axis)
        forward = [(i, i + 1) for i in range(count - 1)]
        backward = [(target, source) for source, target in forward]
        low = lax.ppermute(
            lax.slice_in_dim(block, block.shape[dim] - width, None, axis=dim), axis, forward
        )
        high = lax.ppermute(lax.slice_in_dim(block, 0, width, axis=dim), axis, backward)
        block = jnp.concatenate([low, block, high], axis=dim)
    return block


def local(
    orbitals,
    adjoint_source,
    eigenvalues,
    cell_scale,
    base_potential,
    stiffness,
    face_perm,
    restrict,
    prolong,
    owner,
    pot_slot,
    potential,
):
    nodes = stiffness.shape[0]
    faces = face_perm.shape[1]
    pot_rows = potential.shape[0]
    n_domains = lax.axis_size("dom")
    cell_count = owner.shape[0]
    capacity = 2 * ((cell_count + n_domains - 1) // n_domains)
    onehot = (face_perm[:, :, None] == jnp.arange(faces, dtype=jnp.int32)[None, None, :]).astype(
        jnp.float32
    )

    def assemble_local(partial_sum):
        left_face = partial_sum[:, :, :faces]
        right_face = partial_sum[:, :, nodes - faces :]
        sent_right = jnp.einsum("ckj,cok->coj", onehot, right_face, precision=lax.Precision.HIGHEST)
        boundary = jnp.stack([left_face[0], sent_right[-1]], 0)
        padded = padded_2(boundary, (("dom", 0),), 1)
        left_next = jnp.concatenate([left_face[1:], padded[3][None]], 0)
        add_right = jnp.einsum("ckj,coj->cok", onehot, left_next, precision=lax.Precision.HIGHEST)
        add_left = jnp.concatenate([padded[0][None], sent_right[:-1]], 0)
        return jnp.concatenate(
            [
                left_face + add_left,
                partial_sum[:, :, faces : nodes - faces],
                right_face + add_right,
            ],
            2,
        )

    def operator(values_bf, values_full, shift):
        kinetic = jnp.dot(
            values_bf.reshape(-1, nodes), stiffness, preferred_element_type=jnp.float32
        ).reshape(values_full.shape)
        return assemble_local(cell_scale[:, None, None] * kinetic + shift * values_full)

    source = adjoint_source.astype(jnp.float32)
    shift = base_potential[:, None, :] - eigenvalues[None, :, None]
    iterate = relax * source
    for step_index in range(ITERS):
        image = operator(iterate.astype(jnp.bfloat16), iterate, shift)
        iterate = iterate + relax * (source - image)
    adjoint = iterate.astype(jnp.bfloat16)
    partial_density = jnp.sum(orbitals.astype(jnp.float32) * iterate, axis=1)
    restrict_full = restrict.astype(jnp.float32)
    density_term = lax.psum(partial_density, "orb")
    projected = jnp.dot(density_term, restrict_full, precision=lax.Precision.HIGHEST)
    coarse_cols = projected.shape[1]
    dest_owner = owner[:, 0]
    owner_hot = (dest_owner[:, None] == jnp.arange(n_domains, dtype=jnp.int32)[None, :]).astype(
        jnp.int32
    )
    earlier = jnp.cumsum(owner_hot, axis=0) - owner_hot
    rank_within = jnp.sum(earlier * owner_hot, axis=1)
    slot_index = dest_owner * capacity + rank_within
    send_hot_int = (
        slot_index[None, :] == jnp.arange(n_domains * capacity, dtype=jnp.int32)[:, None]
    ).astype(jnp.int32)
    send_hot = send_hot_int.astype(jnp.float32)
    send_values = jnp.dot(send_hot, projected, precision=lax.Precision.HIGHEST).reshape(
        n_domains, capacity, coarse_cols
    )
    send_ids = (jnp.sum(send_hot_int * (pot_slot + 1)[None, :], axis=1) - 1).reshape(
        n_domains, capacity
    )
    recv_values, recv_ids = (
        lax.all_to_all(send_values, "dom", split_axis=0, concat_axis=0, tiled=True),
        lax.all_to_all(send_ids, "dom", split_axis=0, concat_axis=0, tiled=True),
    )
    recv_hot = (
        recv_ids.reshape(-1)[None, :] == jnp.arange(pot_rows, dtype=jnp.int32)[:, None]
    ).astype(jnp.float32)
    summed = jnp.dot(
        recv_hot, recv_values.reshape(-1, coarse_cols), precision=lax.Precision.HIGHEST
    )
    updated = potential - step_rate * summed
    back_values = jnp.dot(recv_hot.T, updated, precision=lax.Precision.HIGHEST).reshape(
        n_domains, capacity, coarse_cols
    )
    returned = lax.all_to_all(back_values, "dom", split_axis=0, concat_axis=0, tiled=True)
    cell_pot = jnp.dot(
        send_hot.T, returned.reshape(-1, coarse_cols), precision=lax.Precision.HIGHEST
    )
    node_potential = jnp.dot(cell_pot, prolong.astype(jnp.float32), precision=lax.Precision.HIGHEST)
    shift_new = (base_potential + node_potential)[:, None, :]
    applied = operator(orbitals, orbitals.astype(jnp.float32), shift_new).astype(jnp.bfloat16)
    return (adjoint, updated, applied)


def solution(mesh):
    in_specs = (
        P("dom", "orb", None),
        P("dom", "orb", None),
        P("orb"),
        P("dom"),
        P("dom", None),
        P(),
        P("dom", None),
        P(),
        P(),
        P("dom", None),
        P("dom"),
        P("dom", None),
    )
    out_specs = (P("dom", "orb", None), P("dom", None), P("dom", "orb", None))
    return jax.shard_map(local, mesh=mesh, in_specs=in_specs, out_specs=out_specs, check_vma=False)
```

profile of v0, /device:TPU:8, one launch (start us, length us, event | category | flops | bytes accessed | tf_op | source)
XLA Modules:
  0.0 149.7 jit_solution(11445277540518210424)
XLA Ops:
  7.3 1.0 copy-done
  8.2 3.2 %fusion.11 = f32[48,32,512]{2,1,0:T(8,128)S(1)} fusion(bf16[48,32,512]{2,1,0:T(8,128)(2,1)} %param.13, f32[32]{0:T(128)} %param.14, f32[48,512]{1,0:T(8,128)} %param.16, f32[48]{0:T(128)} %param.15, bf16[512,512]{1,0:T(8,128)(2,1)S(1)} %copy-done), kind=kOutput, calls=%fused_computation.22 | convolution fusion | flops 812384256 | bytes 5341504 | tf_op jit(solution)/shard_map/dot_general | solution.py:67
  11.4 4.2 %collective-permute-start.1 = (f32[1,32,64]{2,1,0:T(8,128)S(1)}, f32[1,32,64]{2,1,0:T(8,128)S(1)}, u32[]{:S(2)}, u32[]{:S(2)}) collective-permute-start(f32[1,32,64]{2,1,0:T(8,128)S(1)} %slice.157), channel_id=1, source_target_pairs={{2,0},{4,2},{6,4},{8,6},{10,8},{12,10},{14,12},{16,14},{18,16},{20... | collective-permute-start | bytes 24584 | tf_op jit(solution)/shard_map/ppermute | solution.py:19
  15.7 1.8 %fusion.28 = f32[48,32,64]{2,1,0:T(8,128)S(1)} fusion(s32[48,64]{1,0:T(8,128)S(1)} %copy-done.4, f32[48,32,512]{2,1,0:T(8,128)S(1)} %fusion.11), kind=kOutput, calls=%fused_computation.41 | convolution fusion | flops 75694080 | bytes 1204224 | tf_op jit(solution)/shard_map/ckj,cok->coj/dot_general | solution.py:51
  17.5 1.9 %collective-permute-start = (f32[1,32,64]{2,1,0:T(8,128)S(1)}, f32[1,32,64]{2,1,0:T(8,128)S(1)}, u32[]{:S(2)}, u32[]{:S(2)}) collective-permute-start(f32[1,32,64]{2,1,0:T(8,128)S(1)} %slice.153), channel_id=1, source_target_pairs={{0,2},{2,4},{4,6},{6,8},{8,10},{10,12},{12,14},{14,16},{16,18},{18... | collective-permute-start | bytes 24584 | tf_op jit(solution)/shard_map/ppermute | solution.py:16
  19.9 1.2 slice.156
  21.2 2.7 %slice.155 = f32[48,32,384]{2,1,0:T(8,128)S(1)} slice(f32[48,32,512]{2,1,0:T(8,128)} %copy-done.1), slice={[0:48], [0:32], [64:448]} | slice | bytes 4718592 | tf_op jit(solution)/shard_map/slice | solution.py:60
  23.9 1.5 fusion.30
  25.6 2.8 %fusion.12 = f32[48,32,512]{2,1,0:T(8,128)S(1)} fusion(f32[32]{0:T(128)S(1)} %copy-done.13, f32[48,512]{1,0:T(8,128)S(1)} %copy-done.7, f32[48]{0:T(128)S(1)} %copy-done.14, f32[48,32,64]{2,1,0:T(8,128)S(1)} %fusion.30, f32[48,32,384]{2,1,0:T(8,128)S(1)} %slice.155, f32[48,32,64]{2,1,0:T(8,128)S(1)} %slice_add_fusion.4, ...), kind=kOutput, calls=%fused_computation.23 | convolution fusion | flops 820248576 | bytes 8487232 | tf_op jit(solution)/shard_map/dot_general | solution.py:67
  28.4 5.7 %collective-permute-start.3 = (f32[1,32,64]{2,1,0:T(8,128)S(1)}, f32[1,32,64]{2,1,0:T(8,128)S(1)}, u32[]{:S(2)}, u32[]{:S(2)}) collective-permute-start(f32[1,32,64]{2,1,0:T(8,128)S(1)} %slice.164), channel_id=1, source_target_pairs={{2,0},{4,2},{6,4},{8,6},{10,8},{12,10},{14,12},{16,14},{18,16},{20... | collective-permute-start | bytes 24584 | tf_op jit(solution)/shard_map/ppermute | solution.py:19
  34.1 1.8 %fusion.26 = f32[48,32,64]{2,1,0:T(8,128)S(1)} fusion(s32[48,64]{1,0:T(8,128)S(1)} %copy-done.4, f32[48,32,512]{2,1,0:T(8,128)S(1)} %fusion.12), kind=kOutput, calls=%fused_computation.39 | convolution fusion | flops 75694080 | bytes 1204224 | tf_op jit(solution)/shard_map/ckj,cok->coj/dot_general | solution.py:51
  36.1 0.7 slice.162
  36.8 1.9 %collective-permute-start.2 = (f32[1,32,64]{2,1,0:T(8,128)S(1)}, f32[1,32,64]{2,1,0:T(8,128)S(1)}, u32[]{:S(2)}, u32[]{:S(2)}) collective-permute-start(f32[1,32,64]{2,1,0:T(8,128)S(1)} %slice.160), channel_id=1, source_target_pairs={{0,2},{2,4},{4,6},{6,8},{8,10},{10,12},{12,14},{14,16},{16,18},{18... | collective-permute-start | bytes 24584 | tf_op jit(solution)/shard_map/ppermute | solution.py:16
  38.7 1.4 fusion.31
  40.2 4.0 %collective-permute-done.2 = f32[1,32,64]{2,1,0:T(8,128)S(1)} collective-permute-done((f32[1,32,64]{2,1,0:T(8,128)S(1)}, f32[1,32,64]{2,1,0:T(8,128)S(1)}, u32[]{:S(2)}, u32[]{:S(2)}) %collective-permute-start.2) | collective-permute-done | bytes 8224 | tf_op jit(solution)/shard_map/ppermute | solution.py:16
  44.4 2.8 %fusion.6 = f32[48,32,512]{2,1,0:T(8,128)S(1)} fusion(bf16[48,32,512]{2,1,0:T(8,128)(2,1)S(1)} %copy-done.3, f32[48,32,64]{2,1,0:T(8,128)S(1)} %fusion.31, f32[48,32,384]{2,1,0:T(8,128)S(1)} %slice.162, f32[48,32,64]{2,1,0:T(8,128)S(1)} %slice_add_fusion.3, f32[48,32,64]{2,1,0:T(8,128)S(1)} %fusion.30, f32[48,32,384]{2,1,0:T(8,128)S(1)} %slice.155, ...), kind=kLoop, calls=%fused_computation.17 | loop fusion | flops 9437184 | bytes 11010048 | tf_op jit(solution)/shard_map/add | solution.py:77
  47.3 1.1 fusion.13
  48.4 2.1 %collective-permute-start.5 = (f32[1,32,64]{2,1,0:T(8,128)S(1)}, f32[1,32,64]{2,1,0:T(8,128)S(1)}, u32[]{:S(2)}, u32[]{:S(2)}) collective-permute-start(f32[1,32,64]{2,1,0:T(8,128)S(1)} %slice.171), channel_id=1, source_target_pairs={{2,0},{4,2},{6,4},{8,6},{10,8},{12,10},{14,12},{16,14},{18,16},{20... | collective-permute-start | bytes 24584 | tf_op jit(solution)/shard_map/ppermute | solution.py:19
  50.5 1.8 %fusion.24 = f32[48,32,64]{2,1,0:T(8,128)S(1)} fusion(s32[48,64]{1,0:T(8,128)S(1)} %copy-done.4, f32[48,32,512]{2,1,0:T(8,128)S(1)} %fusion.13), kind=kOutput, calls=%fused_computation.37 | convolution fusion | flops 75694080 | bytes 1204224 | tf_op jit(solution)/shard_map/ckj,cok->coj/dot_general | solution.py:51
  52.5 0.7 slice.169
  53.2 3.9 %collective-permute-start.4 = (f32[1,32,64]{2,1,0:T(8,128)S(1)}, f32[1,32,64]{2,1,0:T(8,128)S(1)}, u32[]{:S(2)}, u32[]{:S(2)}) collective-permute-start(f32[1,32,64]{2,1,0:T(8,128)S(1)} %slice.167), channel_id=1, source_target_pairs={{0,2},{2,4},{4,6},{6,8},{8,10},{10,12},{12,14},{14,16},{16,18},{18... | collective-permute-start | bytes 24584 | tf_op jit(solution)/shard_map/ppermute | solution.py:16
  57.1 1.5 fusion.32
  58.6 2.0 %collective-permute-done.4 = f32[1,32,64]{2,1,0:T(8,128)S(1)} collective-permute-done((f32[1,32,64]{2,1,0:T(8,128)S(1)}, f32[1,32,64]{2,1,0:T(8,128)S(1)}, u32[]{:S(2)}, u32[]{:S(2)}) %collective-permute-start.4) | collective-permute-done | bytes 8224 | tf_op jit(solution)/shard_map/ppermute | solution.py:16
  60.8 2.5 %fusion.14 = f32[48,32,512]{2,1,0:T(8,128)S(1)} fusion(f32[32]{0:T(128)S(1)} %copy-done.13, f32[48,512]{1,0:T(8,128)S(1)} %copy-done.7, f32[48]{0:T(128)S(1)} %copy-done.14, bf16[512,512]{1,0:T(8,128)(2,1)S(1)} %copy-done, f32[48,32,512]{2,1,0:T(8,128)S(1)} %fusion.6, f32[48,32,64]{2,1,0:T(8,128)S(1)} %fusion.32, f32[48,32,384]{2,1,0:T(8,128)S(1)} %slice.169, ...), kind=kOutput, calls=%fused_computation.25 | convolution fusion | flops 818675712 | bytes 11632960 | tf_op jit(solution)/shard_map/dot_general | solution.py:67
  63.2 1.9 %collective-permute-start.7 = (f32[1,32,64]{2,1,0:T(8,128)S(1)}, f32[1,32,64]{2,1,0:T(8,128)S(1)}, u32[]{:S(2)}, u32[]{:S(2)}) collective-permute-start(f32[1,32,64]{2,1,0:T(8,128)S(1)} %slice.178), channel_id=1, source_target_pairs={{2,0},{4,2},{6,4},{8,6},{10,8},{12,10},{14,12},{16,14},{18,16},{20... | collective-permute-start | bytes 24584 | tf_op jit(solution)/shard_map/ppermute | solution.py:19
  65.2 1.8 %fusion.22 = f32[48,32,64]{2,1,0:T(8,128)S(1)} fusion(s32[48,64]{1,0:T(8,128)S(1)} %copy-done.4, f32[48,32,512]{2,1,0:T(8,128)S(1)} %fusion.14), kind=kOutput, calls=%fused_computation.35 | convolution fusion | flops 75694080 | bytes 1204224 | tf_op jit(solution)/shard_map/ckj,cok->coj/dot_general | solution.py:51
  67.2 0.7 slice.176
  67.9 4.1 %collective-permute-start.6 = (f32[1,32,64]{2,1,0:T(8,128)S(1)}, f32[1,32,64]{2,1,0:T(8,128)S(1)}, u32[]{:S(2)}, u32[]{:S(2)}) collective-permute-start(f32[1,32,64]{2,1,0:T(8,128)S(1)} %slice.174), channel_id=1, source_target_pairs={{0,2},{2,4},{4,6},{6,8},{8,10},{10,12},{12,14},{14,16},{16,18},{18... | collective-permute-start | bytes 24584 | tf_op jit(solution)/shard_map/ppermute | solution.py:16
  71.9 1.5 fusion.33
  73.4 2.0 %collective-permute-done.6 = f32[1,32,64]{2,1,0:T(8,128)S(1)} collective-permute-done((f32[1,32,64]{2,1,0:T(8,128)S(1)}, f32[1,32,64]{2,1,0:T(8,128)S(1)}, u32[]{:S(2)}, u32[]{:S(2)}) %collective-permute-start.6) | collective-permute-done | bytes 8224 | tf_op jit(solution)/shard_map/ppermute | solution.py:16
  75.6 4.5 %fusion.2 = (f32[48,512]{1,0:T(8,128)}, bf16[48,32,512]{2,1,0:T(8,128)(2,1)}) fusion(bf16[48,32,512]{2,1,0:T(8,128)(2,1)S(1)} %copy-done.5, f32[48,32,64]{2,1,0:T(8,128)S(1)} %fusion.33, f32[48,32,384]{2,1,0:T(8,128)S(1)} %slice.176, f32[48,32,64]{2,1,0:T(8,128)S(1)} %slice_add_fusion.1, f32[48,32,512]{2,1,0:T(8,128)S(1)} %fusion.6, ...), kind=kLoop, calls=%fused_computation.13 | loop fusion | flops 11771904 | bytes 14254080 | tf_op jit(solution)/shard_map/reduce_sum | solution.py:79
  80.2 0.7 sub.46
  80.9 5.5 %all-to-all-start = ((s32[16,1,6]{2,1,0:T(1,128)}), s32[16,1,6]{2,1,0:T(1,128)S(1)}, u32[]{:S(2)}, u32[]{:S(2)}) async-start(s32[16,1,6]{2,1,0:T(1,128)} %bitcast.2), calls=%async_computation | async-start | bytes 16384 | tf_op jit(solution)/shard_map/all_to_all | solution.py:103
  86.4 11.5 %all-reduce.2.cloned.1.call-done = f32[48,512]{1,0:T(8,128)} async-done(((f32[48,512]{1,0:T(8,128)}), f32[48,512]{1,0:T(8,128)}) %all-reduce.2.cloned.1.call-update) | async-done | bytes 98320 | tf_op jit(solution)/shard_map/psum | solution.py:81
  97.9 1.1 fusion.96
  99.4 0.7 reshape.84
  100.1 7.0 %all-to-all-start.1 = ((f32[16,1,384]{2,1,0:T(1,128)}), f32[16,1,384]{2,1,0:T(1,128)S(1)}, u32[]{:S(2)}, u32[]{:S(2)}) async-start(f32[16,1,384]{2,1,0:T(1,128)} %reshape.84), calls=%async_computation.1 | async-start | bytes 49152 | tf_op jit(solution)/shard_map/all_to_all | solution.py:102
  108.3 4.8 %all-to-all-done.1 = f32[16,1,384]{2,1,0:T(1,128)S(1)} async-done(((f32[16,1,384]{2,1,0:T(1,128)}), f32[16,1,384]{2,1,0:T(1,128)S(1)}, u32[]{:S(2)}, u32[]{:S(2)}) %all-to-all-start.1) | async-done | bytes 24608 | tf_op jit(solution)/shard_map/all_to_all | solution.py:102
  113.6 0.7 reduce.4
  114.9 9.9 %all_to_all.16 = f32[16,1,384]{2,1,0:T(1,128)S(1)} all-to-all(f32[16,1,384]{2,1,0:T(1,128)S(1)} %reshape.86), channel_id=1, replica_groups=mesh['dom'=16,'orb'=2] {'dom'}, dimensions={0} | all-to-all | bytes 49152 | tf_op jit(solution)/shard_map/all_to_all | solution.py:115
  124.9 0.7 reduce.5
  126.1 1.0 fusion.3
  127.1 3.6 %collective-permute-start.9 = (f32[1,32,64]{2,1,0:T(8,128)S(1)}, f32[1,32,64]{2,1,0:T(8,128)S(1)}, u32[]{:S(2)}, u32[]{:S(2)}) collective-permute-start(f32[1,32,64]{2,1,0:T(8,128)S(1)} %slice.185), channel_id=1, source_target_pairs={{2,0},{4,2},{6,4},{8,6},{10,8},{12,10},{14,12},{16,14},{18,16},{20... | collective-permute-start | bytes 24584 | tf_op jit(solution)/shard_map/ppermute | solution.py:19
  130.7 1.8 %fusion.20 = f32[48,32,64]{2,1,0:T(8,128)S(1)} fusion(s32[48,64]{1,0:T(8,128)S(1)} %copy-done.4, f32[48,32,512]{2,1,0:T(8,128)S(1)} %fusion.3), kind=kOutput, calls=%fused_computation.33 | convolution fusion | flops 75694080 | bytes 1204224 | tf_op jit(solution)/shard_map/ckj,cok->coj/dot_general | solution.py:51
  133.2 2.5 %collective-permute-start.8 = (f32[1,32,64]{2,1,0:T(8,128)S(1)}, f32[1,32,64]{2,1,0:T(8,128)S(1)}, u32[]{:S(2)}, u32[]{:S(2)}) collective-permute-start(f32[1,32,64]{2,1,0:T(8,128)S(1)} %slice.181), channel_id=1, source_target_pairs={{0,2},{2,4},{4,6},{6,8},{8,10},{10,12},{12,14},{14,16},{16,18},{18... | collective-permute-start | bytes 24584 | tf_op jit(solution)/shard_map/ppermute | solution.py:16
  135.7 1.7 %fusion.35 = bf16[48,32,64]{2,1,0:T(8,128)(2,1)S(1)} fusion(f32[1,32,64]{2,1,0:T(8,128)S(1)} %collective-permute-done.9, f32[47,32,64]{2,1,0:T(8,128)S(1)} %slice.184, s32[48,64]{1,0:T(8,128)S(1)} %copy-done.4, f32[48,32,512]{2,1,0:T(8,128)S(1)} %fusion.3), kind=kOutput, calls=%fused_computation.48 | convolution fusion | flops 75988992 | bytes 995328 | tf_op jit(solution)/shard_map/ckj,coj->cok/dot_general | solution.py:55
  137.4 3.2 %collective-permute-done.8 = f32[1,32,64]{2,1,0:T(8,128)S(1)} collective-permute-done((f32[1,32,64]{2,1,0:T(8,128)S(1)}, f32[1,32,64]{2,1,0:T(8,128)S(1)}, u32[]{:S(2)}, u32[]{:S(2)}) %collective-permute-start.8) | collective-permute-done | bytes 8224 | tf_op jit(solution)/shard_map/ppermute | solution.py:16
  140.7 2.1 %pad_maximum_fusion = bf16[48,32,512]{2,1,0:T(8,128)(2,1)} fusion(bf16[48,32,64]{2,1,0:T(8,128)(2,1)S(1)} %fusion.35, bf16[48,32,384]{2,1,0:T(8,128)(2,1)S(1)} %slice.209, bf16[48,32,64]{2,1,0:T(8,128)(2,1)S(1)} %fusion.38), kind=kLoop, calls=%fused_computation.27 | loop fusion | flops 4718592 | bytes 3145728 | tf_op jit(solution)/shard_map/concatenate | solution.py:57
  (86 shorter events, 5.6 us)
Async XLA Ops:
  7.2 1.0 copy-start
  7.2 8.5 %copy-start.4 = (s32[48,64]{1,0:T(8,128)S(1)}, s32[48,64]{1,0:T(8,128)}, u32[]{:S(2)}) copy-start(s32[48,64]{1,0:T(8,128)} %param.18) | copy-start | bytes 36868
  7.2 12.2 %copy-start.12 = (s32[48]{0:T(128)S(1)}, s32[48]{0:T(128)}, u32[]{:S(2)}) copy-start(s32[48]{0:T(128)} %param.22) | copy-start | bytes 580
  7.2 12.3 %copy-start.11 = (s32[48,1]{0,1:T(1,128)S(1)}, s32[48,1]{0,1:T(1,128)}, u32[]{:S(2)}) copy-start(s32[48,1]{0,1:T(1,128)} %param.21) | copy-start | bytes 580
  7.2 90.7 %all-reduce.2.cloned.1.call-start = ((), (), s32[]{:S(2)}) async-start(), calls=%async_computation.3 | async-start | bytes 196608 | tf_op jit(solution)/shard_map/psum | solution.py:81
  11.4 4.3 %copy-start.1 = (f32[48,32,512]{2,1,0:T(8,128)}, f32[48,32,512]{2,1,0:T(8,128)S(1)}, u32[]{:S(2)}) copy-start(f32[48,32,512]{2,1,0:T(8,128)S(1)} %fusion.11) | copy-start | bytes 9437188
  11.4 12.5 %collective-permute-start.1 = (f32[1,32,64]{2,1,0:T(8,128)S(1)}, f32[1,32,64]{2,1,0:T(8,128)S(1)}, u32[]{:S(2)}, u32[]{:S(2)}) collective-permute-start(f32[1,32,64]{2,1,0:T(8,128)S(1)} %slice.157), channel_id=1, source_target_pairs={{2,0},{4,2},{6,4},{8,6},{10,8},{12,10},{14,12},{16,14},{18,16},{20... | collective-permute-start | bytes 24584 | tf_op jit(solution)/shard_map/ppermute | solution.py:19
  17.5 7.9 %collective-permute-start = (f32[1,32,64]{2,1,0:T(8,128)S(1)}, f32[1,32,64]{2,1,0:T(8,128)S(1)}, u32[]{:S(2)}, u32[]{:S(2)}) collective-permute-start(f32[1,32,64]{2,1,0:T(8,128)S(1)} %slice.153), channel_id=1, source_target_pairs={{0,2},{2,4},{4,6},{6,8},{8,10},{10,12},{12,14},{14,16},{16,18},{18... | collective-permute-start | bytes 24584 | tf_op jit(solution)/shard_map/ppermute | solution.py:16
  21.1 2.8 %copy-start.2 = (f32[48,32,512]{2,1,0:T(8,128)S(1)}, f32[48,32,512]{2,1,0:T(8,128)}, u32[]{:S(2)}) copy-start(f32[48,32,512]{2,1,0:T(8,128)} %copy-done.1) | copy-start | bytes 9437188
  23.9 1.7 %copy-start.3 = (bf16[48,32,512]{2,1,0:T(8,128)(2,1)S(1)}, bf16[48,32,512]{2,1,0:T(8,128)(2,1)}, u32[]{:S(2)}) copy-start(bf16[48,32,512]{2,1,0:T(8,128)(2,1)} %param.13) | copy-start | bytes 4718596
  23.9 1.7 %copy-start.7 = (f32[48,512]{1,0:T(8,128)S(1)}, f32[48,512]{1,0:T(8,128)}, u32[]{:S(2)}) copy-start(f32[48,512]{1,0:T(8,128)} %param.16) | copy-start | bytes 294916
  23.9 1.7 %copy-start.13 = (f32[32]{0:T(128)S(1)}, f32[32]{0:T(128)}, u32[]{:S(2)}) copy-start(f32[32]{0:T(128)} %param.14) | copy-start | bytes 388
  23.9 1.7 %copy-start.14 = (f32[48]{0:T(128)S(1)}, f32[48]{0:T(128)}, u32[]{:S(2)}) copy-start(f32[48]{0:T(128)} %param.15) | copy-start | bytes 580
  28.4 10.3 %collective-permute-start.3 = (f32[1,32,64]{2,1,0:T(8,128)S(1)}, f32[1,32,64]{2,1,0:T(8,128)S(1)}, u32[]{:S(2)}, u32[]{:S(2)}) collective-permute-start(f32[1,32,64]{2,1,0:T(8,128)S(1)} %slice.164), channel_id=1, source_target_pairs={{2,0},{4,2},{6,4},{8,6},{10,8},{12,10},{14,12},{16,14},{18,16},{20... | collective-permute-start | bytes 24584 | tf_op jit(solution)/shard_map/ppermute | solution.py:19
  36.8 7.4 %collective-permute-start.2 = (f32[1,32,64]{2,1,0:T(8,128)S(1)}, f32[1,32,64]{2,1,0:T(8,128)S(1)}, u32[]{:S(2)}, u32[]{:S(2)}) collective-permute-start(f32[1,32,64]{2,1,0:T(8,128)S(1)} %slice.160), channel_id=1, source_target_pairs={{0,2},{2,4},{4,6},{6,8},{8,10},{10,12},{12,14},{14,16},{16,18},{18... | collective-permute-start | bytes 24584 | tf_op jit(solution)/shard_map/ppermute | solution.py:16
  48.4 8.7 %collective-permute-start.5 = (f32[1,32,64]{2,1,0:T(8,128)S(1)}, f32[1,32,64]{2,1,0:T(8,128)S(1)}, u32[]{:S(2)}, u32[]{:S(2)}) collective-permute-start(f32[1,32,64]{2,1,0:T(8,128)S(1)} %slice.171), channel_id=1, source_target_pairs={{2,0},{4,2},{6,4},{8,6},{10,8},{12,10},{14,12},{16,14},{18,16},{20... | collective-permute-start | bytes 24584 | tf_op jit(solution)/shard_map/ppermute | solution.py:19
  53.2 7.4 %collective-permute-start.4 = (f32[1,32,64]{2,1,0:T(8,128)S(1)}, f32[1,32,64]{2,1,0:T(8,128)S(1)}, u32[]{:S(2)}, u32[]{:S(2)}) collective-permute-start(f32[1,32,64]{2,1,0:T(8,128)S(1)} %slice.167), channel_id=1, source_target_pairs={{0,2},{2,4},{4,6},{6,8},{8,10},{10,12},{12,14},{14,16},{16,18},{18... | collective-permute-start | bytes 24584 | tf_op jit(solution)/shard_map/ppermute | solution.py:16
  63.2 8.7 %collective-permute-start.7 = (f32[1,32,64]{2,1,0:T(8,128)S(1)}, f32[1,32,64]{2,1,0:T(8,128)S(1)}, u32[]{:S(2)}, u32[]{:S(2)}) collective-permute-start(f32[1,32,64]{2,1,0:T(8,128)S(1)} %slice.178), channel_id=1, source_target_pairs={{2,0},{4,2},{6,4},{8,6},{10,8},{12,10},{14,12},{16,14},{18,16},{20... | collective-permute-start | bytes 24584 | tf_op jit(solution)/shard_map/ppermute | solution.py:19
  67.8 7.7 %copy-start.5 = (bf16[48,32,512]{2,1,0:T(8,128)(2,1)S(1)}, bf16[48,32,512]{2,1,0:T(8,128)(2,1)}, u32[]{:S(2)}) copy-start(bf16[48,32,512]{2,1,0:T(8,128)(2,1)} %param.12) | copy-start | bytes 4718596
  67.9 7.6 %collective-permute-start.6 = (f32[1,32,64]{2,1,0:T(8,128)S(1)}, f32[1,32,64]{2,1,0:T(8,128)S(1)}, u32[]{:S(2)}, u32[]{:S(2)}) collective-permute-start(f32[1,32,64]{2,1,0:T(8,128)S(1)} %slice.174), channel_id=1, source_target_pairs={{0,2},{2,4},{4,6},{6,8},{8,10},{10,12},{12,14},{14,16},{16,18},{18... | collective-permute-start | bytes 24584 | tf_op jit(solution)/shard_map/ppermute | solution.py:16
  75.6 22.4 %copy-start.8 = (bf16[512,64]{0,1:T(8,128)(2,1)S(1)}, bf16[512,64]{0,1:T(8,128)(2,1)}, u32[]{:S(2)}) copy-start(bf16[512,64]{0,1:T(8,128)(2,1)} %param.19) | copy-start | bytes 196612
  75.6 38.8 %copy-start.10 = (f32[64,64]{1,0:T(8,128)S(1)}, f32[64,64]{1,0:T(8,128)}, u32[]{:S(2)}) copy-start(f32[64,64]{1,0:T(8,128)} %param.23) | copy-start | bytes 49156
  75.6 50.3 %copy-start.9 = (bf16[64,512]{1,0:T(8,128)(2,1)S(1)}, bf16[64,512]{1,0:T(8,128)(2,1)}, u32[]{:S(2)}) copy-start(bf16[64,512]{1,0:T(8,128)(2,1)} %param.20) | copy-start | bytes 196612
  80.9 19.2 %all-to-all-start = ((s32[16,1,6]{2,1,0:T(1,128)}), s32[16,1,6]{2,1,0:T(1,128)S(1)}, u32[]{:S(2)}, u32[]{:S(2)}) async-start(s32[16,1,6]{2,1,0:T(1,128)} %bitcast.2), calls=%async_computation | async-start | bytes 16384 | tf_op jit(solution)/shard_map/all_to_all | solution.py:103
  100.1 13.0 %all-to-all-start.1 = ((f32[16,1,384]{2,1,0:T(1,128)}), f32[16,1,384]{2,1,0:T(1,128)S(1)}, u32[]{:S(2)}, u32[]{:S(2)}) async-start(f32[16,1,384]{2,1,0:T(1,128)} %reshape.84), calls=%async_computation.1 | async-start | bytes 49152 | tf_op jit(solution)/shard_map/all_to_all | solution.py:102
  114.6 12.6 %copy-start.6 = (f32[64,64]{1,0:T(8,128)}, f32[64,64]{1,0:T(8,128)S(1)}, u32[]{:S(2)}) copy-start(f32[64,64]{1,0:T(8,128)S(1)} %fusion.36) | copy-start | bytes 49156
  127.1 8.5 %collective-permute-start.9 = (f32[1,32,64]{2,1,0:T(8,128)S(1)}, f32[1,32,64]{2,1,0:T(8,128)S(1)}, u32[]{:S(2)}, u32[]{:S(2)}) collective-permute-start(f32[1,32,64]{2,1,0:T(8,128)S(1)} %slice.185), channel_id=1, source_target_pairs={{2,0},{4,2},{6,4},{8,6},{10,8},{12,10},{14,12},{16,14},{18,16},{20... | collective-permute-start | bytes 24584 | tf_op jit(solution)/shard_map/ppermute | solution.py:19
  133.2 7.4 %collective-permute-start.8 = (f32[1,32,64]{2,1,0:T(8,128)S(1)}, f32[1,32,64]{2,1,0:T(8,128)S(1)}, u32[]{:S(2)}, u32[]{:S(2)}) collective-permute-start(f32[1,32,64]{2,1,0:T(8,128)S(1)} %slice.181), channel_id=1, source_target_pairs={{0,2},{2,4},{4,6},{6,8},{8,10},{10,12},{12,14},{14,16},{16,18},{18... | collective-permute-start | bytes 24584 | tf_op jit(solution)/shard_map/ppermute | solution.py:16
Sparse Core Ops, SparseCore 0:
  80.3 17.6 all-reduce.1
where the time goes:
time: 150 us
  starting transfers between devices  44.4 us (30%)
  matrix products  29.3 us (20%)
  waiting for transfers between devices  27.6 us (18%)
  between operations  14.8 us (10%)
  other arithmetic  12.8 us (9%)
  local copies, waits for them, and re-layouts  10.9 us (7%)
  blocking collectives  9.95 us (7%)
    ppermute x5, starting transfers between devices, padded_2(): lax.ppermute(lax.slice_in_dim(block, 0, width, axis=dim), axis, backward)  17.6 us
    ppermute x5, starting transfers between devices, padded_2(): lax.ppermute(lax.slice_in_dim(block, block.shape[dim] - width, None, axis...  14.3 us
    psum x1, waiting for transfers between devices, local(): density_term = lax.psum(partial_density, 'orb')  11.5 us
    ppermute x5, waiting for transfers between devices, padded_2(): lax.ppermute(lax.slice_in_dim(block, block.shape[dim] - width, None, axis...  11.3 us
    dot_general x5, matrix products, operator(): jnp.dot(values_bf.reshape(-1, nodes), stiffness, preferred_element_type=j...  10.6 us
    all_to_all x1, blocking collectives, local(): lax.all_to_all(back_values, 'dom', split_axis=0, concat_axis=0, tiled=True)  9.95 us
    dot_general x5, matrix products, assemble_local(): jnp.einsum('ckj,cok->coj', onehot, right_face, precision=lax.Precision.HI...  9.03 us
    dot_general x5, matrix products, assemble_local(): jnp.einsum('ckj,coj->cok', onehot, left_next, precision=lax.Precision.HIG...  7.53 us
  transfers between devices with their start and end apart: 13, of which 6 were waited for; matrix products, arithmetic and copies ran while one was open for 19% of the time, Pallas kernels for 0%

commit v1 on v0

--- a/solution.py
+++ b/solution.py
@@ -78,7 +78,7 @@
     adjoint = iterate.astype(jnp.bfloat16)
     partial_density = jnp.sum(orbitals.astype(jnp.float32) * iterate, axis=1)
     restrict_full = restrict.astype(jnp.float32)
-    density_term = lax.psum(partial_density, "orb")
+    density_term = jnp.sum(lax.all_gather(partial_density, "orb"), axis=0)
     projected = jnp.dot(density_term, restrict_full, precision=lax.Precision.HIGHEST)
     coarse_cols = projected.shape[1]
     dest_owner = owner[:, 0]

time: 150 us -> 124 us (0.83)
  between operations: 14.8 us -> 1.34 us
  waiting for transfers between devices: 27.6 us -> 17.5 us
  local copies, waits for them, and re-layouts: 10.9 us -> 6.79 us
  blocking collectives: 9.95 us -> 11.9 us
  starting transfers between devices: 44.4 us -> 42.6 us
    psum x1 -> x0, waiting for transfers between devices: 11.5 us -> none  [local(): density_term = lax.psum(partial_density, 'orb')]
    ppermute x5, starting transfers between devices: 17.6 us -> 14.1 us  [padded_2(): lax.ppermute(lax.slice_in_dim(block, 0, width, axis=dim), axis, backward)]
    slice x5, local copies, waits for them, and re-layouts: 5.15 us -> 3.12 us  [assemble_local(): partial_sum[:, :, faces:nodes - faces]]
    all_gather x0 -> x1, blocking collectives: none -> 1.93 us  [local(): density_term = jnp.sum(lax.all_gather(partial_density, 'orb'), axis=0)]
    ppermute x5, starting transfers between devices: 14.3 us -> 16 us  [padded_2(): lax.ppermute(lax.slice_in_dim(block, block.shape[dim] - width, None, axis...]
    all_to_all x1, starting transfers between devices: 5.55 us -> 7.22 us  [local(): lax.all_to_all(send_ids, 'dom', split_axis=0, concat_axis=0, tiled=True)]
    all_to_all x1, starting transfers between devices: 6.97 us -> 5.32 us  [local(): lax.all_to_all(send_values, 'dom', split_axis=0, concat_axis=0, tiled=True)]
  transfers between devices with their start and end apart: 13 -> 12, of which waited for: 6 -> 6; matrix products, arithmetic and copies ran while one was open for 19% -> 33% of each run, Pallas kernels for 0% -> 0%
where the time goes in v1:
time: 124 us; the launch traced here: 123 us
  starting transfers between devices  42.6 us (34%)
  matrix products  28.9 us (23%)
  waiting for transfers between devices  17.5 us (14%)
  other arithmetic  14.2 us (11%)
  blocking collectives  11.9 us (10%)
  local copies, waits for them, and re-layouts  6.79 us (5%)
  between operations  1.34 us (1%)
    ppermute x5, starting transfers between devices, padded_2(): lax.ppermute(lax.slice_in_dim(block, block.shape[dim] - width, None, axis...  16 us
    ppermute x5, starting transfers between devices, padded_2(): lax.ppermute(lax.slice_in_dim(block, 0, width, axis=dim), axis, backward)  14.1 us
    ppermute x5, waiting for transfers between devices, padded_2(): lax.ppermute(lax.slice_in_dim(block, block.shape[dim] - width, None, axis...  12.7 us
    dot_general x5, matrix products, operator(): jnp.dot(values_bf.reshape(-1, nodes), stiffness, preferred_element_type=j...  11 us
    all_to_all x1, blocking collectives, local(): lax.all_to_all(back_values, 'dom', split_axis=0, concat_axis=0, tiled=True)  9.95 us
    dot_general x5, matrix products, assemble_local(): jnp.einsum('ckj,cok->coj', onehot, right_face, precision=lax.Precision.HI...  9.03 us
    dot_general x5, matrix products, assemble_local(): jnp.einsum('ckj,coj->cok', onehot, left_next, precision=lax.Precision.HIG...  7.57 us
    all_to_all x1, starting transfers between devices, local(): lax.all_to_all(send_ids, 'dom', split_axis=0, concat_axis=0, tiled=True)  7.22 us
  transfers between devices with their start and end apart: 12, of which 6 were waited for; matrix products, arithmetic and copies ran while one was open for 33% of the time, Pallas kernels for 0%

profile of v1, /device:TPU:8, one launch (start us, length us, event | category | flops | bytes accessed | tf_op | source)
XLA Modules:
  0.0 123.1 jit_solution(17083634524664530923)
XLA Ops:
  0.6 0.8 fusion.81
  1.5 0.8 select_reduce_fusion.1
  2.3 0.7 multiply_add_fusion
  3.1 0.7 sub.46
  3.8 7.2 %all-to-all-start = ((s32[16,1,6]{2,1,0:T(1,128)}), s32[16,1,6]{2,1,0:T(1,128)S(1)}, u32[]{:S(2)}, u32[]{:S(2)}) async-start(s32[16,1,6]{2,1,0:T(1,128)} %bitcast.2), calls=%async_computation | async-start | bytes 16384 | tf_op jit(solution)/shard_map/all_to_all | solution.py:103
  11.1 3.3 %fusion.11 = f32[48,32,512]{2,1,0:T(8,128)S(1)} fusion(bf16[48,32,512]{2,1,0:T(8,128)(2,1)} %param.13, f32[32]{0:T(128)} %param.14, f32[48,512]{1,0:T(8,128)} %param.16, f32[48]{0:T(128)} %param.15, bf16[512,512]{1,0:T(8,128)(2,1)S(1)} %copy-done), kind=kOutput, calls=%fused_computation.22 | convolution fusion | flops 812384256 | bytes 5341504 | tf_op jit(solution)/shard_map/dot_general | solution.py:67
  14.4 4.3 %collective-permute-start.1 = (f32[1,32,64]{2,1,0:T(8,128)S(1)}, f32[1,32,64]{2,1,0:T(8,128)S(1)}, u32[]{:S(2)}, u32[]{:S(2)}) collective-permute-start(f32[1,32,64]{2,1,0:T(8,128)S(1)} %slice.157), channel_id=1, source_target_pairs={{2,0},{4,2},{6,4},{8,6},{10,8},{12,10},{14,12},{16,14},{18,16},{20... | collective-permute-start | bytes 24584 | tf_op jit(solution)/shard_map/ppermute | solution.py:19
  18.7 1.8 %fusion.28 = f32[48,32,64]{2,1,0:T(8,128)S(1)} fusion(s32[48,64]{1,0:T(8,128)S(1)} %copy-done.2, f32[48,32,512]{2,1,0:T(8,128)S(1)} %fusion.11), kind=kOutput, calls=%fused_computation.41 | convolution fusion | flops 75694080 | bytes 1204224 | tf_op jit(solution)/shard_map/ckj,cok->coj/dot_general | solution.py:51
  20.5 1.9 %collective-permute-start = (f32[1,32,64]{2,1,0:T(8,128)S(1)}, f32[1,32,64]{2,1,0:T(8,128)S(1)}, u32[]{:S(2)}, u32[]{:S(2)}) collective-permute-start(f32[1,32,64]{2,1,0:T(8,128)S(1)} %slice.153), channel_id=1, source_target_pairs={{0,2},{2,4},{4,6},{6,8},{8,10},{10,12},{12,14},{14,16},{16,18},{18... | collective-permute-start | bytes 24584 | tf_op jit(solution)/shard_map/ppermute | solution.py:16
  22.6 0.7 slice.155
  23.3 1.5 %fusion.30 = f32[48,32,64]{2,1,0:T(8,128)S(1)} fusion(f32[1,32,64]{2,1,0:T(8,128)S(1)} %collective-permute-done.1, f32[47,32,64]{2,1,0:T(8,128)S(1)} %slice.156, s32[48,64]{1,0:T(8,128)S(1)} %copy-done.2, f32[48,32,512]{2,1,0:T(8,128)S(1)} %fusion.11), kind=kOutput, calls=%fused_computation.43 | convolution fusion | flops 75890688 | bytes 1191936 | tf_op jit(solution)/shard_map/ckj,coj->cok/dot_general | solution.py:55
  24.8 3.1 %collective-permute-done = f32[1,32,64]{2,1,0:T(8,128)S(1)} collective-permute-done((f32[1,32,64]{2,1,0:T(8,128)S(1)}, f32[1,32,64]{2,1,0:T(8,128)S(1)}, u32[]{:S(2)}, u32[]{:S(2)}) %collective-permute-start) | collective-permute-done | bytes 8224 | tf_op jit(solution)/shard_map/ppermute | solution.py:16
  28.1 2.8 %fusion.12 = f32[48,32,512]{2,1,0:T(8,128)S(1)} fusion(f32[32]{0:T(128)S(1)} %copy-done.9, f32[48,512]{1,0:T(8,128)S(1)} %copy-done.5, f32[48]{0:T(128)S(1)} %copy-done.10, f32[48,32,64]{2,1,0:T(8,128)S(1)} %fusion.30, f32[48,32,384]{2,1,0:T(8,128)S(1)} %slice.155, f32[48,32,64]{2,1,0:T(8,128)S(1)} %slice_add_fusion.4, ...), kind=kOutput, calls=%fused_computation.23 | convolution fusion | flops 820248576 | bytes 8487232 | tf_op jit(solution)/shard_map/dot_general | solution.py:67
  30.9 2.6 %collective-permute-start.3 = (f32[1,32,64]{2,1,0:T(8,128)S(1)}, f32[1,32,64]{2,1,0:T(8,128)S(1)}, u32[]{:S(2)}, u32[]{:S(2)}) collective-permute-start(f32[1,32,64]{2,1,0:T(8,128)S(1)} %slice.164), channel_id=1, source_target_pairs={{2,0},{4,2},{6,4},{8,6},{10,8},{12,10},{14,12},{16,14},{18,16},{20... | collective-permute-start | bytes 24584 | tf_op jit(solution)/shard_map/ppermute | solution.py:19
  33.5 1.8 %fusion.26 = f32[48,32,64]{2,1,0:T(8,128)S(1)} fusion(s32[48,64]{1,0:T(8,128)S(1)} %copy-done.2, f32[48,32,512]{2,1,0:T(8,128)S(1)} %fusion.12), kind=kOutput, calls=%fused_computation.39 | convolution fusion | flops 75694080 | bytes 1204224 | tf_op jit(solution)/shard_map/ckj,cok->coj/dot_general | solution.py:51
  35.5 0.7 slice.162
  36.2 3.4 %collective-permute-start.2 = (f32[1,32,64]{2,1,0:T(8,128)S(1)}, f32[1,32,64]{2,1,0:T(8,128)S(1)}, u32[]{:S(2)}, u32[]{:S(2)}) collective-permute-start(f32[1,32,64]{2,1,0:T(8,128)S(1)} %slice.160), channel_id=1, source_target_pairs={{0,2},{2,4},{4,6},{6,8},{8,10},{10,12},{12,14},{14,16},{16,18},{18... | collective-permute-start | bytes 24584 | tf_op jit(solution)/shard_map/ppermute | solution.py:16
  39.7 1.5 %fusion.31 = f32[48,32,64]{2,1,0:T(8,128)S(1)} fusion(f32[1,32,64]{2,1,0:T(8,128)S(1)} %collective-permute-done.3, f32[47,32,64]{2,1,0:T(8,128)S(1)} %slice.163, s32[48,64]{1,0:T(8,128)S(1)} %copy-done.2, f32[48,32,512]{2,1,0:T(8,128)S(1)} %fusion.12), kind=kOutput, calls=%fused_computation.44 | convolution fusion | flops 75890688 | bytes 1191936 | tf_op jit(solution)/shard_map/ckj,coj->cok/dot_general | solution.py:55
  41.1 2.5 %collective-permute-done.2 = f32[1,32,64]{2,1,0:T(8,128)S(1)} collective-permute-done((f32[1,32,64]{2,1,0:T(8,128)S(1)}, f32[1,32,64]{2,1,0:T(8,128)S(1)}, u32[]{:S(2)}, u32[]{:S(2)}) %collective-permute-start.2) | collective-permute-done | bytes 8224 | tf_op jit(solution)/shard_map/ppermute | solution.py:16
  43.8 2.9 %fusion.6 = f32[48,32,512]{2,1,0:T(8,128)S(1)} fusion(bf16[48,32,512]{2,1,0:T(8,128)(2,1)S(1)} %copy-done.1, f32[48,32,64]{2,1,0:T(8,128)S(1)} %fusion.31, f32[48,32,384]{2,1,0:T(8,128)S(1)} %slice.162, f32[48,32,64]{2,1,0:T(8,128)S(1)} %slice_add_fusion.3, f32[48,32,64]{2,1,0:T(8,128)S(1)} %fusion.30, f32[48,32,384]{2,1,0:T(8,128)S(1)} %slice.155, ...), kind=kLoop, calls=%fused_computation.17 | loop fusion | flops 9437184 | bytes 11010048 | tf_op jit(solution)/shard_map/add | solution.py:77
  46.7 1.1 fusion.13
  47.8 1.9 %collective-permute-start.5 = (f32[1,32,64]{2,1,0:T(8,128)S(1)}, f32[1,32,64]{2,1,0:T(8,128)S(1)}, u32[]{:S(2)}, u32[]{:S(2)}) collective-permute-start(f32[1,32,64]{2,1,0:T(8,128)S(1)} %slice.171), channel_id=1, source_target_pairs={{2,0},{4,2},{6,4},{8,6},{10,8},{12,10},{14,12},{16,14},{18,16},{20... | collective-permute-start | bytes 24584 | tf_op jit(solution)/shard_map/ppermute | solution.py:19
  49.8 1.8 %fusion.24 = f32[48,32,64]{2,1,0:T(8,128)S(1)} fusion(s32[48,64]{1,0:T(8,128)S(1)} %copy-done.2, f32[48,32,512]{2,1,0:T(8,128)S(1)} %fusion.13), kind=kOutput, calls=%fused_computation.37 | convolution fusion | flops 75694080 | bytes 1204224 | tf_op jit(solution)/shard_map/ckj,cok->coj/dot_general | solution.py:51
  51.8 0.7 slice.169
  52.4 3.9 %collective-permute-start.4 = (f32[1,32,64]{2,1,0:T(8,128)S(1)}, f32[1,32,64]{2,1,0:T(8,128)S(1)}, u32[]{:S(2)}, u32[]{:S(2)}) collective-permute-start(f32[1,32,64]{2,1,0:T(8,128)S(1)} %slice.167), channel_id=1, source_target_pairs={{0,2},{2,4},{4,6},{6,8},{8,10},{10,12},{12,14},{14,16},{16,18},{18... | collective-permute-start | bytes 24584 | tf_op jit(solution)/shard_map/ppermute | solution.py:16
  56.4 1.5 %fusion.32 = f32[48,32,64]{2,1,0:T(8,128)S(1)} fusion(f32[1,32,64]{2,1,0:T(8,128)S(1)} %collective-permute-done.5, f32[47,32,64]{2,1,0:T(8,128)S(1)} %slice.170, s32[48,64]{1,0:T(8,128)S(1)} %copy-done.2, f32[48,32,512]{2,1,0:T(8,128)S(1)} %fusion.13), kind=kOutput, calls=%fused_computation.45 | convolution fusion | flops 75890688 | bytes 1191936 | tf_op jit(solution)/shard_map/ckj,coj->cok/dot_general | solution.py:55
  57.8 2.0 %collective-permute-done.4 = f32[1,32,64]{2,1,0:T(8,128)S(1)} collective-permute-done((f32[1,32,64]{2,1,0:T(8,128)S(1)}, f32[1,32,64]{2,1,0:T(8,128)S(1)}, u32[]{:S(2)}, u32[]{:S(2)}) %collective-permute-start.4) | collective-permute-done | bytes 8224 | tf_op jit(solution)/shard_map/ppermute | solution.py:16
  60.0 2.7 %fusion.14 = f32[48,32,512]{2,1,0:T(8,128)S(1)} fusion(f32[32]{0:T(128)S(1)} %copy-done.9, f32[48,512]{1,0:T(8,128)S(1)} %copy-done.5, f32[48]{0:T(128)S(1)} %copy-done.10, bf16[512,512]{1,0:T(8,128)(2,1)S(1)} %copy-done, f32[48,32,512]{2,1,0:T(8,128)S(1)} %fusion.6, f32[48,32,64]{2,1,0:T(8,128)S(1)} %fusion.32, f32[48,32,384]{2,1,0:T(8,128)S(1)} %slice.169, ...), kind=kOutput, calls=%fused_computation.25 | convolution fusion | flops 818675712 | bytes 11632960 | tf_op jit(solution)/shard_map/dot_general | solution.py:67
  62.8 1.9 %collective-permute-start.7 = (f32[1,32,64]{2,1,0:T(8,128)S(1)}, f32[1,32,64]{2,1,0:T(8,128)S(1)}, u32[]{:S(2)}, u32[]{:S(2)}) collective-permute-start(f32[1,32,64]{2,1,0:T(8,128)S(1)} %slice.178), channel_id=1, source_target_pairs={{2,0},{4,2},{6,4},{8,6},{10,8},{12,10},{14,12},{16,14},{18,16},{20... | collective-permute-start | bytes 24584 | tf_op jit(solution)/shard_map/ppermute | solution.py:19
  64.7 1.8 %fusion.22 = f32[48,32,64]{2,1,0:T(8,128)S(1)} fusion(s32[48,64]{1,0:T(8,128)S(1)} %copy-done.2, f32[48,32,512]{2,1,0:T(8,128)S(1)} %fusion.14), kind=kOutput, calls=%fused_computation.35 | convolution fusion | flops 75694080 | bytes 1204224 | tf_op jit(solution)/shard_map/ckj,cok->coj/dot_general | solution.py:51
  67.4 4.3 %collective-permute-start.6 = (f32[1,32,64]{2,1,0:T(8,128)S(1)}, f32[1,32,64]{2,1,0:T(8,128)S(1)}, u32[]{:S(2)}, u32[]{:S(2)}) collective-permute-start(f32[1,32,64]{2,1,0:T(8,128)S(1)} %slice.174), channel_id=1, source_target_pairs={{0,2},{2,4},{4,6},{6,8},{8,10},{10,12},{12,14},{14,16},{16,18},{18... | collective-permute-start | bytes 24584 | tf_op jit(solution)/shard_map/ppermute | solution.py:16
  71.7 1.5 %fusion.33 = f32[48,32,64]{2,1,0:T(8,128)S(1)} fusion(f32[1,32,64]{2,1,0:T(8,128)S(1)} %collective-permute-done.7, f32[47,32,64]{2,1,0:T(8,128)S(1)} %slice.177, s32[48,64]{1,0:T(8,128)S(1)} %copy-done.2, f32[48,32,512]{2,1,0:T(8,128)S(1)} %fusion.14), kind=kOutput, calls=%fused_computation.46 | convolution fusion | flops 75890688 | bytes 1191936 | tf_op jit(solution)/shard_map/ckj,coj->cok/dot_general | solution.py:55
  73.1 1.8 %collective-permute-done.6 = f32[1,32,64]{2,1,0:T(8,128)S(1)} collective-permute-done((f32[1,32,64]{2,1,0:T(8,128)S(1)}, f32[1,32,64]{2,1,0:T(8,128)S(1)}, u32[]{:S(2)}, u32[]{:S(2)}) %collective-permute-start.6) | collective-permute-done | bytes 8224 | tf_op jit(solution)/shard_map/ppermute | solution.py:16
  75.1 3.9 %fusion.2 = (f32[48,512]{1,0:T(8,128)S(1)}, bf16[48,32,512]{2,1,0:T(8,128)(2,1)}) fusion(bf16[48,32,512]{2,1,0:T(8,128)(2,1)S(1)} %copy-done.3, f32[48,32,64]{2,1,0:T(8,128)S(1)} %fusion.33, f32[48,32,384]{2,1,0:T(8,128)S(1)} %slice.176, f32[48,32,64]{2,1,0:T(8,128)S(1)} %slice_add_fusion.1, f32[48,32,512]{2,1,0:T(8,128)S(1)} %fusion.6, ...), kind=kLoop, calls=%fused_computation.13 | loop fusion | flops 11771904 | bytes 14254080 | tf_op jit(solution)/shard_map/reduce_sum | solution.py:79
  79.0 1.9 %all-gather = f32[96,512]{1,0:T(8,128)S(1)} all-gather(f32[48,512]{1,0:T(8,128)S(1)} %get-tuple-element.3), channel_id=2, replica_groups=mesh['dom'=16,'orb'=2] {'orb'}, dimensions={0}, use_global_device_ids=true | all-gather | bytes 294912 | tf_op jit(solution)/shard_map/all_gather | solution.py:81
  81.5 0.7 reshape.85
  82.2 5.3 %all-to-all-start.1 = ((f32[16,1,384]{2,1,0:T(1,128)}), f32[16,1,384]{2,1,0:T(1,128)S(1)}, u32[]{:S(2)}, u32[]{:S(2)}) async-start(f32[16,1,384]{2,1,0:T(1,128)} %reshape.85), calls=%async_computation.1 | async-start | bytes 49152 | tf_op jit(solution)/shard_map/all_to_all | solution.py:102
  88.8 4.8 %all-to-all-done.1 = f32[16,1,384]{2,1,0:T(1,128)S(1)} async-done(((f32[16,1,384]{2,1,0:T(1,128)}), f32[16,1,384]{2,1,0:T(1,128)S(1)}, u32[]{:S(2)}, u32[]{:S(2)}) %all-to-all-start.1) | async-done | bytes 24608 | tf_op jit(solution)/shard_map/all_to_all | solution.py:102
  94.1 0.7 reduce.4
  95.4 9.9 %all_to_all.16 = f32[16,1,384]{2,1,0:T(1,128)S(1)} all-to-all(f32[16,1,384]{2,1,0:T(1,128)S(1)} %reshape.87), channel_id=1, replica_groups=mesh['dom'=16,'orb'=2] {'dom'}, dimensions={0} | all-to-all | bytes 49152 | tf_op jit(solution)/shard_map/all_to_all | solution.py:115
  105.4 0.7 reduce.5
  106.6 1.0 fusion.3
  107.6 3.4 %collective-permute-start.9 = (f32[1,32,64]{2,1,0:T(8,128)S(1)}, f32[1,32,64]{2,1,0:T(8,128)S(1)}, u32[]{:S(2)}, u32[]{:S(2)}) collective-permute-start(f32[1,32,64]{2,1,0:T(8,128)S(1)} %slice.185), channel_id=1, source_target_pairs={{2,0},{4,2},{6,4},{8,6},{10,8},{12,10},{14,12},{16,14},{18,16},{20... | collective-permute-start | bytes 24584 | tf_op jit(solution)/shard_map/ppermute | solution.py:19
  111.0 1.8 %fusion.20 = f32[48,32,64]{2,1,0:T(8,128)S(1)} fusion(s32[48,64]{1,0:T(8,128)S(1)} %copy-done.2, f32[48,32,512]{2,1,0:T(8,128)S(1)} %fusion.3), kind=kOutput, calls=%fused_computation.33 | convolution fusion | flops 75694080 | bytes 1204224 | tf_op jit(solution)/shard_map/ckj,cok->coj/dot_general | solution.py:51
  113.4 2.5 %collective-permute-start.8 = (f32[1,32,64]{2,1,0:T(8,128)S(1)}, f32[1,32,64]{2,1,0:T(8,128)S(1)}, u32[]{:S(2)}, u32[]{:S(2)}) collective-permute-start(f32[1,32,64]{2,1,0:T(8,128)S(1)} %slice.181), channel_id=1, source_target_pairs={{0,2},{2,4},{4,6},{6,8},{8,10},{10,12},{12,14},{14,16},{16,18},{18... | collective-permute-start | bytes 24584 | tf_op jit(solution)/shard_map/ppermute | solution.py:16
  115.9 1.7 %fusion.35 = bf16[48,32,64]{2,1,0:T(8,128)(2,1)S(1)} fusion(f32[1,32,64]{2,1,0:T(8,128)S(1)} %collective-permute-done.9, f32[47,32,64]{2,1,0:T(8,128)S(1)} %slice.184, s32[48,64]{1,0:T(8,128)S(1)} %copy-done.2, f32[48,32,512]{2,1,0:T(8,128)S(1)} %fusion.3), kind=kOutput, calls=%fused_computation.48 | convolution fusion | flops 75988992 | bytes 995328 | tf_op jit(solution)/shard_map/ckj,coj->cok/dot_general | solution.py:55
  117.7 3.2 %collective-permute-done.8 = f32[1,32,64]{2,1,0:T(8,128)S(1)} collective-permute-done((f32[1,32,64]{2,1,0:T(8,128)S(1)}, f32[1,32,64]{2,1,0:T(8,128)S(1)}, u32[]{:S(2)}, u32[]{:S(2)}) %collective-permute-start.8) | collective-permute-done | bytes 8224 | tf_op jit(solution)/shard_map/ppermute | solution.py:16
  121.0 2.1 %pad_maximum_fusion = bf16[48,32,512]{2,1,0:T(8,128)(2,1)} fusion(bf16[48,32,64]{2,1,0:T(8,128)(2,1)S(1)} %fusion.35, bf16[48,32,384]{2,1,0:T(8,128)(2,1)S(1)} %slice.209, bf16[48,32,64]{2,1,0:T(8,128)(2,1)S(1)} %fusion.38), kind=kLoop, calls=%fused_computation.27 | loop fusion | flops 4718592 | bytes 3145728 | tf_op jit(solution)/shard_map/concatenate | solution.py:57
  (76 shorter events, 6.3 us)
Async XLA Ops:
  0.6 10.4 %copy-start = (bf16[512,512]{1,0:T(8,128)(2,1)S(1)}, bf16[512,512]{1,0:T(8,128)(2,1)}, u32[]{:S(2)}) copy-start(bf16[512,512]{1,0:T(8,128)(2,1)} %param.17) | copy-start | bytes 1572868
  3.8 78.4 %all-to-all-start = ((s32[16,1,6]{2,1,0:T(1,128)}), s32[16,1,6]{2,1,0:T(1,128)S(1)}, u32[]{:S(2)}, u32[]{:S(2)}) async-start(s32[16,1,6]{2,1,0:T(1,128)} %bitcast.2), calls=%async_computation | async-start | bytes 16384 | tf_op jit(solution)/shard_map/all_to_all | solution.py:103
  11.1 7.6 %copy-start.2 = (s32[48,64]{1,0:T(8,128)S(1)}, s32[48,64]{1,0:T(8,128)}, u32[]{:S(2)}) copy-start(s32[48,64]{1,0:T(8,128)} %param.18) | copy-start | bytes 36868
  14.4 8.9 %collective-permute-start.1 = (f32[1,32,64]{2,1,0:T(8,128)S(1)}, f32[1,32,64]{2,1,0:T(8,128)S(1)}, u32[]{:S(2)}, u32[]{:S(2)}) collective-permute-start(f32[1,32,64]{2,1,0:T(8,128)S(1)} %slice.157), channel_id=1, source_target_pairs={{2,0},{4,2},{6,4},{8,6},{10,8},{12,10},{14,12},{16,14},{18,16},{20... | collective-permute-start | bytes 24584 | tf_op jit(solution)/shard_map/ppermute | solution.py:19
  20.5 7.4 %collective-permute-start = (f32[1,32,64]{2,1,0:T(8,128)S(1)}, f32[1,32,64]{2,1,0:T(8,128)S(1)}, u32[]{:S(2)}, u32[]{:S(2)}) collective-permute-start(f32[1,32,64]{2,1,0:T(8,128)S(1)} %slice.153), channel_id=1, source_target_pairs={{0,2},{2,4},{4,6},{6,8},{8,10},{10,12},{12,14},{14,16},{16,18},{18... | collective-permute-start | bytes 24584 | tf_op jit(solution)/shard_map/ppermute | solution.py:16
  23.3 4.8 %copy-start.1 = (bf16[48,32,512]{2,1,0:T(8,128)(2,1)S(1)}, bf16[48,32,512]{2,1,0:T(8,128)(2,1)}, u32[]{:S(2)}) copy-start(bf16[48,32,512]{2,1,0:T(8,128)(2,1)} %param.13) | copy-start | bytes 4718596
  23.3 4.8 %copy-start.5 = (f32[48,512]{1,0:T(8,128)S(1)}, f32[48,512]{1,0:T(8,128)}, u32[]{:S(2)}) copy-start(f32[48,512]{1,0:T(8,128)} %param.16) | copy-start | bytes 294916
  23.3 4.8 %copy-start.9 = (f32[32]{0:T(128)S(1)}, f32[32]{0:T(128)}, u32[]{:S(2)}) copy-start(f32[32]{0:T(128)} %param.14) | copy-start | bytes 388
  23.3 4.8 %copy-start.10 = (f32[48]{0:T(128)S(1)}, f32[48]{0:T(128)}, u32[]{:S(2)}) copy-start(f32[48]{0:T(128)} %param.15) | copy-start | bytes 580
  30.9 8.7 %collective-permute-start.3 = (f32[1,32,64]{2,1,0:T(8,128)S(1)}, f32[1,32,64]{2,1,0:T(8,128)S(1)}, u32[]{:S(2)}, u32[]{:S(2)}) collective-permute-start(f32[1,32,64]{2,1,0:T(8,128)S(1)} %slice.164), channel_id=1, source_target_pairs={{2,0},{4,2},{6,4},{8,6},{10,8},{12,10},{14,12},{16,14},{18,16},{20... | collective-permute-start | bytes 24584 | tf_op jit(solution)/shard_map/ppermute | solution.py:19
  36.2 7.4 %collective-permute-start.2 = (f32[1,32,64]{2,1,0:T(8,128)S(1)}, f32[1,32,64]{2,1,0:T(8,128)S(1)}, u32[]{:S(2)}, u32[]{:S(2)}) collective-permute-start(f32[1,32,64]{2,1,0:T(8,128)S(1)} %slice.160), channel_id=1, source_target_pairs={{0,2},{2,4},{4,6},{6,8},{8,10},{10,12},{12,14},{14,16},{16,18},{18... | collective-permute-start | bytes 24584 | tf_op jit(solution)/shard_map/ppermute | solution.py:16
  47.8 8.5 %collective-permute-start.5 = (f32[1,32,64]{2,1,0:T(8,128)S(1)}, f32[1,32,64]{2,1,0:T(8,128)S(1)}, u32[]{:S(2)}, u32[]{:S(2)}) collective-permute-start(f32[1,32,64]{2,1,0:T(8,128)S(1)} %slice.171), channel_id=1, source_target_pairs={{2,0},{4,2},{6,4},{8,6},{10,8},{12,10},{14,12},{16,14},{18,16},{20... | collective-permute-start | bytes 24584 | tf_op jit(solution)/shard_map/ppermute | solution.py:19
  52.4 7.4 %collective-permute-start.4 = (f32[1,32,64]{2,1,0:T(8,128)S(1)}, f32[1,32,64]{2,1,0:T(8,128)S(1)}, u32[]{:S(2)}, u32[]{:S(2)}) collective-permute-start(f32[1,32,64]{2,1,0:T(8,128)S(1)} %slice.167), channel_id=1, source_target_pairs={{0,2},{2,4},{4,6},{6,8},{8,10},{10,12},{12,14},{14,16},{16,18},{18... | collective-permute-start | bytes 24584 | tf_op jit(solution)/shard_map/ppermute | solution.py:16
  62.8 8.9 %collective-permute-start.7 = (f32[1,32,64]{2,1,0:T(8,128)S(1)}, f32[1,32,64]{2,1,0:T(8,128)S(1)}, u32[]{:S(2)}, u32[]{:S(2)}) collective-permute-start(f32[1,32,64]{2,1,0:T(8,128)S(1)} %slice.178), channel_id=1, source_target_pairs={{2,0},{4,2},{6,4},{8,6},{10,8},{12,10},{14,12},{16,14},{18,16},{20... | collective-permute-start | bytes 24584 | tf_op jit(solution)/shard_map/ppermute | solution.py:19
  67.4 7.7 %copy-start.3 = (bf16[48,32,512]{2,1,0:T(8,128)(2,1)S(1)}, bf16[48,32,512]{2,1,0:T(8,128)(2,1)}, u32[]{:S(2)}) copy-start(bf16[48,32,512]{2,1,0:T(8,128)(2,1)} %param.12) | copy-start | bytes 4718596
  67.4 7.6 %collective-permute-start.6 = (f32[1,32,64]{2,1,0:T(8,128)S(1)}, f32[1,32,64]{2,1,0:T(8,128)S(1)}, u32[]{:S(2)}, u32[]{:S(2)}) collective-permute-start(f32[1,32,64]{2,1,0:T(8,128)S(1)} %slice.174), channel_id=1, source_target_pairs={{0,2},{2,4},{4,6},{6,8},{8,10},{10,12},{12,14},{14,16},{16,18},{18... | collective-permute-start | bytes 24584 | tf_op jit(solution)/shard_map/ppermute | solution.py:16
  75.1 5.9 %copy-start.6 = (bf16[512,64]{0,1:T(8,128)(2,1)S(1)}, bf16[512,64]{0,1:T(8,128)(2,1)}, u32[]{:S(2)}) copy-start(bf16[512,64]{0,1:T(8,128)(2,1)} %param.19) | copy-start | bytes 196612
  75.1 19.8 %copy-start.8 = (f32[64,64]{1,0:T(8,128)S(1)}, f32[64,64]{1,0:T(8,128)}, u32[]{:S(2)}) copy-start(f32[64,64]{1,0:T(8,128)} %param.23) | copy-start | bytes 49156
  75.1 31.2 %copy-start.7 = (bf16[64,512]{1,0:T(8,128)(2,1)S(1)}, bf16[64,512]{1,0:T(8,128)(2,1)}, u32[]{:S(2)}) copy-start(bf16[64,512]{1,0:T(8,128)(2,1)} %param.20) | copy-start | bytes 196612
  82.2 11.4 %all-to-all-start.1 = ((f32[16,1,384]{2,1,0:T(1,128)}), f32[16,1,384]{2,1,0:T(1,128)S(1)}, u32[]{:S(2)}, u32[]{:S(2)}) async-start(f32[16,1,384]{2,1,0:T(1,128)} %reshape.85), calls=%async_computation.1 | async-start | bytes 49152 | tf_op jit(solution)/shard_map/all_to_all | solution.py:102
  95.0 12.6 %copy-start.4 = (f32[64,64]{1,0:T(8,128)}, f32[64,64]{1,0:T(8,128)S(1)}, u32[]{:S(2)}) copy-start(f32[64,64]{1,0:T(8,128)S(1)} %fusion.36) | copy-start | bytes 49156
  107.6 8.3 %collective-permute-start.9 = (f32[1,32,64]{2,1,0:T(8,128)S(1)}, f32[1,32,64]{2,1,0:T(8,128)S(1)}, u32[]{:S(2)}, u32[]{:S(2)}) collective-permute-start(f32[1,32,64]{2,1,0:T(8,128)S(1)} %slice.185), channel_id=1, source_target_pairs={{2,0},{4,2},{6,4},{8,6},{10,8},{12,10},{14,12},{16,14},{18,16},{20... | collective-permute-start | bytes 24584 | tf_op jit(solution)/shard_map/ppermute | solution.py:19
  113.4 7.4 %collective-permute-start.8 = (f32[1,32,64]{2,1,0:T(8,128)S(1)}, f32[1,32,64]{2,1,0:T(8,128)S(1)}, u32[]{:S(2)}, u32[]{:S(2)}) collective-permute-start(f32[1,32,64]{2,1,0:T(8,128)S(1)} %slice.181), channel_id=1, source_target_pairs={{0,2},{2,4},{4,6},{6,8},{8,10},{10,12},{12,14},{14,16},{16,18},{18... | collective-permute-start | bytes 24584 | tf_op jit(solution)/shard_map/ppermute | solution.py:16
